TPU v7x, 256 devices: a whole 4x4x8 slice. The times are simulated.
256 devices in a mesh: dp: 8 (over z), bin: 32 (over x, y, core).
Axes of the slice: x: 4, y: 4, z: 8, core: 2. Of those that a mesh axis runs over, the one named last changes fastest.
Arguments:
- embeddings: bfloat16 [196608, 256], P(('dp', 'bin')), may hold values from -8 to 8
- bin_ids: int32 [196608], P(('dp', 'bin')), may hold values from 0 to 31, as said below
- spreads: float32 [3], replicated, may hold values from 0.5 to 4
- projection: bfloat16 [256, 256], replicated, may hold values from -0.375 to 0.375
Outputs:
- grad_emb: bfloat16 [196608, 256], P(('dp', 'bin'))
- grad_w: float32 [256, 256], replicated
- loss: float32 [], replicated
Inputs may be any that keep to these rules, and one draw needn't show every extreme that they name: `bin_ids`: among the 768 jets of one device at most 48 share a mass bin, and on every device one bin holds exactly 48 of them.
All inputs are finite; a program needn't handle non-finite values.
Results may differ from a plain program's by a relative error of at most 0.0044.
The roundings to bfloat16 on the way count: a program that leaves them out, or rounds other values in their place, can miss the bound.
Values may be sent and summed in bfloat16 or wider, within the bound.
A program may use at most 64 MiB of HBM per device.

v0:
```python
import jax
import jax.numpy as jnp
from jax import lax
from jax.sharding import PartitionSpec as P


def from_partner(value, axis, bit):
    mask = 2**bit
    pairs = [(source, source ^ mask) for source in range(lax.axis_size(axis))]
    return lax.ppermute(value, axis, pairs)


def tile_terms(xa, mask_a, xb, mask_b, inv_bw):
    rows_a, width = xa.shape
    rows_b = xb.shape[0]
    block = 512
    count = rows_a // block
    sq_b = jnp.sum(jnp.square(xb.astype(jnp.float32)), 1)
    coef = inv_bw / width

    def step(carry, item):
        total, col_sum, back = carry
        xblk, mblk = item
        inner = lax.dot_general(
            xblk, xb, (((1,), (1,)), ((), ())), preferred_element_type=jnp.float32
        )
        sq_a = jnp.sum(jnp.square(xblk.astype(jnp.float32)), 1)
        dist = sq_a[:, None] + sq_b[None, :] - 2.0 * inner
        kern = jnp.zeros(dist.shape, jnp.float32)
        weight = jnp.zeros(dist.shape, jnp.float32)
        for index in range(coef.shape[0]):
            expo = jnp.exp(-dist * coef[index])
            kern = kern + expo
            weight = weight + coef[index] * expo
        pairs = mblk[:, None] * mask_b[None, :]
        total = total + jnp.sum(kern * pairs)
        gram = (weight * pairs).astype(jnp.bfloat16)
        gram_f = gram.astype(jnp.float32)
        part_a = xblk.astype(jnp.float32) * jnp.sum(gram_f, 1)[:, None] - jnp.dot(
            gram, xb, preferred_element_type=jnp.float32
        )
        return ((total, col_sum, back), part_a)

    init = (
        jnp.zeros((), jnp.float32),
        jnp.zeros((rows_b,), jnp.float32),
        jnp.zeros((rows_b, width), jnp.float32),
    )
    (total, col_sum, back), parts = lax.scan(
        step, init, (xa.reshape(count, block, width), mask_a.reshape(count, block))
    )
    part_a = parts.reshape(rows_a, width)
    part_b = xb.astype(jnp.float32) * col_sum[:, None] - back
    return (total, part_a, part_b)


def local(embeddings, bin_ids, spreads, projection):
    rows, width = embeddings.shape
    owners = lax.axis_size("bin")
    slots_per = 2 * rows // owners
    inv_bw = 1.0 / spreads
    feats = jnp.dot(embeddings, projection, preferred_element_type=jnp.float32).astype(jnp.bfloat16)
    onehot = (bin_ids[:, None] == jnp.arange(owners, dtype=jnp.int32)[None, :]).astype(jnp.int32)
    counts = jnp.sum(onehot, 0)
    slot = jnp.sum((jnp.cumsum(onehot, 0) - 1) * onehot, 1)
    outbox = jnp.zeros((owners, slots_per, width), jnp.bfloat16).at[bin_ids, slot].set(feats)
    inbox, arrived = (
        lax.all_to_all(outbox, "bin", split_axis=0, concat_axis=0, tiled=True),
        lax.all_to_all(counts[:, None], "bin", split_axis=0, concat_axis=0, tiled=True),
    )
    mine = inbox.reshape(owners * slots_per, width)
    slot_ids = jnp.arange(slots_per, dtype=jnp.int32)[None, :]
    live = (slot_ids < arrived).astype(jnp.float32).reshape(-1)
    own_n = jnp.maximum(jnp.sum(arrived).astype(jnp.float32), 1.0)
    bit = owners.bit_length() - 2
    partner, partner_arrived = from_partner((mine, arrived), "bin", bit)
    partner_live = (slot_ids < partner_arrived).astype(jnp.float32).reshape(-1)
    partner_n = jnp.maximum(jnp.sum(partner_arrived).astype(jnp.float32), 1.0)
    self_sum, self_part, unused = tile_terms(mine, live, mine, live, inv_bw)
    cross_sum, cross_part, spare = tile_terms(mine, live, partner, partner_live, inv_bw)
    cross_loss = -cross_sum / (own_n * partner_n)
    scale = float(rows * width)
    grad_feat = (
        scale * (-(4.0 / (own_n * own_n)) * self_part + 4.0 / (own_n * partner_n) * cross_part)
    ).astype(jnp.bfloat16)
    local_loss = self_sum / (own_n * own_n) + cross_loss
    homeward = lax.all_to_all(
        grad_feat.reshape(owners, slots_per, width), "bin", split_axis=0, concat_axis=0, tiled=True
    )
    grad_rows = homeward[bin_ids, slot]
    grad_emb = lax.dot_general(
        grad_rows, projection, (((1,), (1,)), ((), ())), preferred_element_type=jnp.float32
    ).astype(jnp.bfloat16)
    partial_w = lax.dot_general(
        embeddings, grad_rows, (((0,), (0,)), ((), ())), preferred_element_type=jnp.float32
    )
    replicas = lax.axis_size("dp")
    tokens_all = float(rows * replicas * owners)
    loss_sum = lax.psum(local_loss, ("dp", "bin"))
    weight_sum = lax.psum(partial_w, ("dp", "bin"))
    return (grad_emb, weight_sum / tokens_all, loss_sum / replicas)


def solution(mesh):
    return jax.shard_map(
        local,
        mesh=mesh,
        in_specs=(P(("dp", "bin"), None), P(("dp", "bin")), P(), P()),
        out_specs=(P(("dp", "bin"), None), P(), P()),
        check_vma=False,
    )
```

profile of v0, /device:TPU:2, one launch (start us, length us, event | category | flops | bytes accessed | tf_op | source)
XLA Modules:
  0.0 560.4 jit_solution(6354406823277336630)
XLA Ops:
  7.9 1.7 reduce-window.6
  11.6 7.6 %all-to-all-start = ((s32[32,1,1]{2,1,0:T(1,128)}), s32[32,1,1]{2,1,0:T(1,128)S(1)}, u32[]{:S(2)}, u32[]{:S(2)}) async-start(s32[32,1,1]{2,1,0:T(1,128)} %copy.13), calls=%async_computation | async-start | bytes 32768 | tf_op jit(solution)/shard_map/all_to_all | solution.py:69
  22.1 83.9 %scatter_fusion = bf16[32,48,256]{2,1,0:T(8,128)(2,1)} fusion(bf16[32,48,256]{2,1,0:T(8,128)(2,1)} %broadcast_in_dim.10, s32[768]{0:T(1024)S(1)} %get-tuple-element.160, bf16[768,256]{1,0:T(8,128)(2,1)S(1)} %convolution_convert_fusion.1), kind=kCustom, calls=%fused_computation.1 | custom fusion | bytes 1185792 | tf_op jit(solution)/shard_map/scatter | solution.py:66
  105.9 8.0 %all-to-all-start.1 = ((bf16[32,48,256]{2,1,0:T(8,128)(2,1)}), bf16[32,48,256]{2,1,0:T(8,128)(2,1)}, u32[]{:S(2)}, u32[]{:S(2)}) async-start(bf16[32,48,256]{2,1,0:T(8,128)(2,1)} %scatter_fusion), calls=%async_computation.1 | async-start | bytes 1572864 | tf_op jit(solution)/shard_map/all_to_all | solution.py:68
  115.3 2.2 collective-permute-start
  118.2 7.4 %collective-permute-done = s32[32,1]{0,1:T(1,128)S(1)} collective-permute-done((s32[32,1]{0,1:T(1,128)S(1)}, s32[32,1]{0,1:T(1,128)S(1)}, u32[]{:S(2)}, u32[]{:S(2)}) %collective-permute-start) | collective-permute-done | bytes 160 | tf_op jit(solution)/shard_map/ppermute | solution.py:10
  127.0 1.7 collective-permute-start.1
  130.3 33.9 %while.26 = (s32[]{:T(128)}, f32[]{:T(128)}, f32[3,512,256]{2,1,0:T(8,128)S(1)}, bf16[3,512,256]{2,1,0:T(8,128)(2,1)}, f32[1536]{0:T(1024)S(1)}, /*index=5*/bf16...) while((s32[]{:T(128)}, f32[]{:T(128)}, ...), condition=%wide.region_11.12_spmd.clone, body=%wide.region_7.11_spmd.clone.sunk | while | flops 822609920 | bytes 6076697 | solution.py:49
  132.3 7.0 %convert_reduce_fusion.5 = (f32[512]{0:T(512)S(1)}, bf16[512,1536]{1,0:T(8,128)(2,1)S(1)}, f32[]{:T(128)}) fusion(f32[1536]{0:T(1024)S(1)} %mul.351, f32[512]{0:T(512)S(1)} %bitcast.112, f32[]{:T(128)} %bitcast.97, f32[]{:T(128)} %bitcast.98, f32[]{:T(128)} %bitcast.99, bf16[1536,256]{1,0:T(8,128)(2,1)} %get-tuple-element.400, ...), kind=kOutput, calls=%fused_computation.11.clone.1 | convolution fusion | flops 419167744 | bytes 2641924 | tf_op jit(solution)/shard_map/while/body/eval_jaxpr/dot_general | solution.py:24
  139.2 1.8 fusion.70
  143.6 7.0 %convert_reduce_fusion.5 = (f32[512]{0:T(512)S(1)}, bf16[512,1536]{1,0:T(8,128)(2,1)S(1)}, f32[]{:T(128)}) fusion(f32[1536]{0:T(1024)S(1)} %mul.351, f32[512]{0:T(512)S(1)} %bitcast.112, f32[]{:T(128)} %bitcast.97, f32[]{:T(128)} %bitcast.98, f32[]{:T(128)} %bitcast.99, bf16[1536,256]{1,0:T(8,128)(2,1)} %get-tuple-element.400, ...), kind=kOutput, calls=%fused_computation.11.clone.1 | convolution fusion | flops 419167744 | bytes 2641924 | tf_op jit(solution)/shard_map/while/body/eval_jaxpr/dot_general | solution.py:24
  150.5 1.8 fusion.70
  154.9 7.0 %convert_reduce_fusion.5 = (f32[512]{0:T(512)S(1)}, bf16[512,1536]{1,0:T(8,128)(2,1)S(1)}, f32[]{:T(128)}) fusion(f32[1536]{0:T(1024)S(1)} %mul.351, f32[512]{0:T(512)S(1)} %bitcast.112, f32[]{:T(128)} %bitcast.97, f32[]{:T(128)} %bitcast.98, f32[]{:T(128)} %bitcast.99, bf16[1536,256]{1,0:T(8,128)(2,1)} %get-tuple-element.400, ...), kind=kOutput, calls=%fused_computation.11.clone.1 | convolution fusion | flops 419167744 | bytes 2641924 | tf_op jit(solution)/shard_map/while/body/eval_jaxpr/dot_general | solution.py:24
  161.8 1.8 fusion.70
  165.3 42.6 %while.27 = (s32[]{:T(128)}, f32[]{:T(128)}, f32[3,512,256]{2,1,0:T(8,128)S(1)}, bf16[3,512,256]{2,1,0:T(8,128)(2,1)}, f32[1536]{0:T(1024)}, /*index=5*/bf16[153...) while((s32[]{:T(128)}, f32[]{:T(128)}, ...), condition=%wide.region_18.19_spmd.clone, body=%wide.region_14.18_spmd.clone.sunk | while | flops 822609920 | bytes 9273709 | solution.py:49
  165.3 1.7 fusion.76
  170.4 6.9 %convert_reduce_fusion.6 = (f32[512]{0:T(512)S(1)}, bf16[512,1536]{1,0:T(8,128)(2,1)S(1)}, f32[]{:T(128)}) fusion(f32[1536]{0:T(1024)S(1)} %mul.354, f32[512]{0:T(512)} %bitcast.113, f32[]{:T(128)} %bitcast.108, f32[]{:T(128)} %bitcast.109, f32[]{:T(128)} %bitcast.110, bf16[1536,256]{1,0:T(8,128)(2,1)} %get-tuple-element.370, ...), kind=kOutput, calls=%fused_computation.34.clone.1 | convolution fusion | flops 419167744 | bytes 2643972 | tf_op jit(solution)/shard_map/while/body/eval_jaxpr/dot_general | solution.py:24
  184.6 6.9 %convert_reduce_fusion.6 = (f32[512]{0:T(512)S(1)}, bf16[512,1536]{1,0:T(8,128)(2,1)S(1)}, f32[]{:T(128)}) fusion(f32[1536]{0:T(1024)S(1)} %mul.354, f32[512]{0:T(512)} %bitcast.113, f32[]{:T(128)} %bitcast.108, f32[]{:T(128)} %bitcast.109, f32[]{:T(128)} %bitcast.110, bf16[1536,256]{1,0:T(8,128)(2,1)} %get-tuple-element.370, ...), kind=kOutput, calls=%fused_computation.34.clone.1 | convolution fusion | flops 419167744 | bytes 2643972 | tf_op jit(solution)/shard_map/while/body/eval_jaxpr/dot_general | solution.py:24
  193.7 1.7 fusion.76
  198.8 6.9 %convert_reduce_fusion.6 = (f32[512]{0:T(512)S(1)}, bf16[512,1536]{1,0:T(8,128)(2,1)S(1)}, f32[]{:T(128)}) fusion(f32[1536]{0:T(1024)S(1)} %mul.354, f32[512]{0:T(512)} %bitcast.113, f32[]{:T(128)} %bitcast.108, f32[]{:T(128)} %bitcast.109, f32[]{:T(128)} %bitcast.110, bf16[1536,256]{1,0:T(8,128)(2,1)} %get-tuple-element.370, ...), kind=kOutput, calls=%fused_computation.34.clone.1 | convolution fusion | flops 419167744 | bytes 2643972 | tf_op jit(solution)/shard_map/while/body/eval_jaxpr/dot_general | solution.py:24
  209.1 7.4 %all-to-all-start.2 = ((bf16[32,48,256]{2,1,0:T(8,128)(2,1)}), bf16[32,48,256]{2,1,0:T(8,128)(2,1)S(1)}, u32[]{:S(2)}, u32[]{:S(2)}) async-start(bf16[32,48,256]{2,1,0:T(8,128)(2,1)} %bitcast.111), calls=%async_computation.2 | async-start | bytes 1572864 | tf_op jit(solution)/shard_map/all_to_all | solution.py:87
  216.6 80.5 %psum.15 = f32[]{:T(128)} all-reduce(f32[]{:T(128)S(6)} %add.95), channel_id=1, replica_groups=mesh['dp'=8,'bin'=32] {'dp','bin'}, use_global_device_ids=true, to_apply=%region_20.21 | all-reduce | flops 1 | bytes 8 | tf_op jit(solution)/shard_map/psum | solution.py:99
  297.8 4.4 gather_fusion
  304.4 246.2 %all-reduce.2.cloned.1.call-done = f32[256,256]{0,1:T(8,128)} async-done(((f32[256,256]{0,1:T(8,128)}), f32[256,256]{0,1:T(8,128)}) %all-reduce.2.cloned.1.call-update) | async-done | bytes 262160 | tf_op jit(solution)/shard_map/psum | solution.py:100
  (89 shorter events, 37.4 us)
Async XLA Ops:
  7.2 12.8 %copy-start = (bf16[768,256]{1,0:T(8,128)(2,1)S(1)}, bf16[768,256]{1,0:T(8,128)(2,1)}, u32[]{:S(2)}) copy-start(bf16[768,256]{1,0:T(8,128)(2,1)} %param.8) | copy-start | bytes 1179652
  11.6 94.4 %all-to-all-start = ((s32[32,1,1]{2,1,0:T(1,128)}), s32[32,1,1]{2,1,0:T(1,128)S(1)}, u32[]{:S(2)}, u32[]{:S(2)}) async-start(s32[32,1,1]{2,1,0:T(1,128)} %copy.13), calls=%async_computation | async-start | bytes 32768 | tf_op jit(solution)/shard_map/all_to_all | solution.py:69
  105.9 8.0 %copy-start.7 = (f32[3]{0:T(128)S(1)}, f32[3]{0:T(128)}, u32[]{:S(2)}) copy-start(f32[3]{0:T(128)} %param.10) | copy-start | bytes 40
  105.9 21.0 %all-to-all-start.1 = ((bf16[32,48,256]{2,1,0:T(8,128)(2,1)}), bf16[32,48,256]{2,1,0:T(8,128)(2,1)}, u32[]{:S(2)}, u32[]{:S(2)}) async-start(bf16[32,48,256]{2,1,0:T(8,128)(2,1)} %scatter_fusion), calls=%async_computation.1 | async-start | bytes 1572864 | tf_op jit(solution)/shard_map/all_to_all | solution.py:68
  115.3 10.3 %collective-permute-start = (s32[32,1]{0,1:T(1,128)S(1)}, s32[32,1]{0,1:T(1,128)S(1)}, u32[]{:S(2)}, u32[]{:S(2)}) collective-permute-start(s32[32,1]{0,1:T(1,128)S(1)} %bitcast.115), channel_id=1, source_target_pairs={{0,16},{1,17},{2,18},{3,19},{4,20},{5,21},{6,22},{7,23},{8,24},{9,... | collective-permute-start | bytes 392 | tf_op jit(solution)/shard_map/ppermute | solution.py:10
  125.6 4.7 copy-start.6
  127.0 37.3 %collective-permute-start.1 = (bf16[1536,256]{1,0:T(8,128)(2,1)}, bf16[1536,256]{1,0:T(8,128)(2,1)S(1)}, u32[]{:S(2)}, u32[]{:S(2)}) collective-permute-start(bf16[1536,256]{1,0:T(8,128)(2,1)} %bitcast.4), channel_id=1, source_target_pairs={{0,16},{1,17},{2,18},{3,19},{4,20},{5,21},{6,22},{7,23},{8,24},{9,... | collective-permute-start | bytes 2359304 | tf_op jit(solution)/shard_map/ppermute | solution.py:10
  164.3 0.9 copy-start.1
  165.3 2.9 copy-start.4
  170.4 6.9 %copy-start.2 = (bf16[1536,256]{1,0:T(8,128)(2,1)S(1)}, bf16[1536,256]{1,0:T(8,128)(2,1)}, u32[]{:S(2)}) copy-start(bf16[1536,256]{1,0:T(8,128)(2,1)} %get-tuple-element.370) | copy-start | bytes 2359300 | tf_op jit(solution)/shard_map/while
  177.3 2.2 copy-start.5
  179.5 2.9 copy-start.4
  184.6 7.0 %copy-start.2 = (bf16[1536,256]{1,0:T(8,128)(2,1)S(1)}, bf16[1536,256]{1,0:T(8,128)(2,1)}, u32[]{:S(2)}) copy-start(bf16[1536,256]{1,0:T(8,128)(2,1)} %get-tuple-element.370) | copy-start | bytes 2359300 | tf_op jit(solution)/shard_map/while
  191.5 2.2 copy-start.5
  193.7 2.9 copy-start.4
  198.8 7.0 %copy-start.2 = (bf16[1536,256]{1,0:T(8,128)(2,1)S(1)}, bf16[1536,256]{1,0:T(8,128)(2,1)}, u32[]{:S(2)}) copy-start(bf16[1536,256]{1,0:T(8,128)(2,1)} %get-tuple-element.370) | copy-start | bytes 2359300 | tf_op jit(solution)/shard_map/while
  205.7 2.2 copy-start.5
  209.1 88.7 %all-to-all-start.2 = ((bf16[32,48,256]{2,1,0:T(8,128)(2,1)}), bf16[32,48,256]{2,1,0:T(8,128)(2,1)S(1)}, u32[]{:S(2)}, u32[]{:S(2)}) async-start(bf16[32,48,256]{2,1,0:T(8,128)(2,1)} %bitcast.111), calls=%async_computation.2 | async-start | bytes 1572864 | tf_op jit(solution)/shard_map/all_to_all | solution.py:87
  216.5 334.1 %all-reduce.2.cloned.1.call-start = ((), (), s32[]{:S(2)}) async-start(), calls=%async_computation.3 | async-start | bytes 524288 | tf_op jit(solution)/shard_map/psum | solution.py:100
  297.8 5.5 copy-start.3
Sparse Core Ops, SparseCore 0:
  303.4 247.0 all-reduce.1
where the time goes:
time: 564 us; the launch traced here: 560 us
  waiting for transfers between devices  254 us (45%)
  local copies, waits for them, and re-layouts  99.8 us (18%)
  blocking collectives  80.5 us (14%)
  matrix products  54.8 us (10%)
  starting transfers between devices  26.9 us (5%)
  other arithmetic  23.1 us (4%)
  between operations  17.5 us (3%)
    psum x1, waiting for transfers between devices, local(): weight_sum = lax.psum(partial_w, ('dp', 'bin'))  246 us
    scatter x1, local copies, waits for them, and re-layouts, local(): jnp.zeros((owners, slots_per, width), jnp.bfloat16).at[bin_ids, slot]  83.9 us
    psum x1, blocking collectives, local(): loss_sum = lax.psum(local_loss, ('dp', 'bin'))  80.5 us
    dot_general x6, matrix products, step(): lax.dot_general(xblk, xb, (((1,), (1,)), ((), ())), preferred_element_typ...  41.7 us
  transfers between devices with their start and end apart: 6, of which 2 were waited for; matrix products, arithmetic and copies ran while one was open for 22% of the time, Pallas kernels for 0%

commit v1 on v0

--- a/solution.py
+++ b/solution.py
@@ -97,7 +97,9 @@
     replicas = lax.axis_size("dp")
     tokens_all = float(rows * replicas * owners)
     loss_sum = lax.psum(local_loss, ("dp", "bin"))
-    weight_sum = lax.psum(partial_w, ("dp", "bin"))
+    weight_sum = partial_w
+    for mesh_axis in ("dp", "bin"):
+        weight_sum = lax.psum(weight_sum, mesh_axis)
     return (grad_emb, weight_sum / tokens_all, loss_sum / replicas)
 
 

time: 564 us -> 442 us (0.78)
  waiting for transfers between devices: 254 us -> 113 us
  blocking collectives: 80.5 us -> 98.8 us
  matrix products: 54.8 us -> 64.3 us
  starting transfers between devices: 26.9 us -> 19 us
    psum x1 -> x2, waiting for transfers between devices: 246 us -> 106 us  [local(): weight_sum = lax.psum(weight_sum, mesh_axis)]
    all_to_all x0 -> x1, blocking collectives: none -> 19.2 us  [local(): lax.all_to_all(grad_feat.reshape(owners, slots_per, width), 'bin', split_...]
    all_to_all x1 -> x0, starting transfers between devices: 7.39 us -> none  [local(): lax.all_to_all(grad_feat.reshape(owners, slots_per, width), 'bin', split_...]
    dot_general x6, matrix products: 41.7 us -> 47.6 us  [step(): lax.dot_general(xblk, xb, (((1,), (1,)), ((), ())), preferred_element_typ...]
  transfers between devices with their start and end apart: 6 -> 6, of which waited for: 2 -> 2; matrix products, arithmetic and copies ran while one was open for 22% -> 29% of each run, Pallas kernels for 0% -> 0%
where the time goes in v1:
time: 442 us; the launch traced here: 437 us
  waiting for transfers between devices  113 us (26%)
  local copies, waits for them, and re-layouts  102 us (23%)
  blocking collectives  98.8 us (22%)
  matrix products  64.3 us (15%)
  starting transfers between devices  19 us (4%)
  other arithmetic  18.5 us (4%)
  between operations  17.5 us (4%)
    psum x2, waiting for transfers between devices, local(): weight_sum = lax.psum(weight_sum, mesh_axis)  106 us
    scatter x1, local copies, waits for them, and re-layouts, local(): jnp.zeros((owners, slots_per, width), jnp.bfloat16).at[bin_ids, slot]  84.2 us
    psum x1, blocking collectives, local(): loss_sum = lax.psum(local_loss, ('dp', 'bin'))  79.6 us
    dot_general x6, matrix products, step(): lax.dot_general(xblk, xb, (((1,), (1,)), ((), ())), preferred_element_typ...  47.6 us
    all_to_all x1, blocking collectives, local(): lax.all_to_all(grad_feat.reshape(owners, slots_per, width), 'bin', split_...  19.2 us
    dot_general x6, matrix products, step(): jnp.dot(gram, xb, preferred_element_type=jnp.float32)  13.5 us
  transfers between devices with their start and end apart: 6, of which 2 were waited for; matrix products, arithmetic and copies ran while one was open for 29% of the time, Pallas kernels for 0%

profile of v1, /device:TPU:2, one launch (start us, length us, event | category | flops | bytes accessed | tf_op | source)
XLA Modules:
  0.0 437.4 jit_solution(935200264774674997)
XLA Ops:
  7.9 1.7 reduce-window.6
  11.6 7.6 %all-to-all-start = ((s32[32,1,1]{2,1,0:T(1,128)}), s32[32,1,1]{2,1,0:T(1,128)S(1)}, u32[]{:S(2)}, u32[]{:S(2)}) async-start(s32[32,1,1]{2,1,0:T(1,128)} %copy.13), calls=%async_computation | async-start | bytes 32768 | tf_op jit(solution)/shard_map/all_to_all | solution.py:69
  22.0 84.2 %scatter_fusion = bf16[32,48,256]{2,1,0:T(8,128)(2,1)} fusion(bf16[32,48,256]{2,1,0:T(8,128)(2,1)} %broadcast_in_dim.10, s32[768]{0:T(1024)S(1)} %get-tuple-element.160, bf16[768,256]{1,0:T(8,128)(2,1)S(1)} %convolution_convert_fusion.1), kind=kCustom, calls=%fused_computation.1 | custom fusion | bytes 1185792 | tf_op jit(solution)/shard_map/scatter | solution.py:66
  106.3 7.4 %all-to-all-start.1 = ((bf16[32,48,256]{2,1,0:T(8,128)(2,1)}), bf16[32,48,256]{2,1,0:T(8,128)(2,1)}, u32[]{:S(2)}, u32[]{:S(2)}) async-start(bf16[32,48,256]{2,1,0:T(8,128)(2,1)} %scatter_fusion), calls=%async_computation.1 | async-start | bytes 1572864 | tf_op jit(solution)/shard_map/all_to_all | solution.py:68
  115.1 2.2 collective-permute-start
  118.0 7.4 %collective-permute-done = s32[32,1]{0,1:T(1,128)S(1)} collective-permute-done((s32[32,1]{0,1:T(1,128)S(1)}, s32[32,1]{0,1:T(1,128)S(1)}, u32[]{:S(2)}, u32[]{:S(2)}) %collective-permute-start) | collective-permute-done | bytes 160 | tf_op jit(solution)/shard_map/ppermute | solution.py:10
  130.1 38.2 %while.26 = (s32[]{:T(128)}, f32[]{:T(128)}, f32[3,512,256]{2,1,0:T(8,128)S(1)}, bf16[3,512,256]{2,1,0:T(8,128)(2,1)}, f32[1536]{0:T(1024)S(1)}, /*index=5*/bf16...) while((s32[]{:T(128)}, f32[]{:T(128)}, ...), condition=%wide.region_11.12_spmd.clone, body=%wide.region_7.11_spmd.clone.sunk | while | flops 822609920 | bytes 6076197 | solution.py:49
  132.0 8.0 %convert_reduce_fusion.5 = (f32[512]{0:T(512)S(1)}, bf16[512,1536]{1,0:T(8,128)(2,1)}, f32[]{:T(128)}) fusion(f32[1536]{0:T(1024)S(1)} %mul.351, f32[512]{0:T(512)S(1)} %bitcast.112, f32[]{:T(128)} %bitcast.97, f32[]{:T(128)} %bitcast.98, f32[]{:T(128)} %bitcast.99, bf16[1536,256]{1,0:T(8,128)(2,1)} %get-tuple-element.400, ...), kind=kOutput, calls=%fused_computation.11.clone.1 | convolution fusion | flops 419167744 | bytes 2641416 | tf_op jit(solution)/shard_map/while/body/eval_jaxpr/dot_general | solution.py:24
  140.6 2.2 fusion.70
  144.7 8.0 %convert_reduce_fusion.5 = (f32[512]{0:T(512)S(1)}, bf16[512,1536]{1,0:T(8,128)(2,1)}, f32[]{:T(128)}) fusion(f32[1536]{0:T(1024)S(1)} %mul.351, f32[512]{0:T(512)S(1)} %bitcast.112, f32[]{:T(128)} %bitcast.97, f32[]{:T(128)} %bitcast.98, f32[]{:T(128)} %bitcast.99, bf16[1536,256]{1,0:T(8,128)(2,1)} %get-tuple-element.400, ...), kind=kOutput, calls=%fused_computation.11.clone.1 | convolution fusion | flops 419167744 | bytes 2641416 | tf_op jit(solution)/shard_map/while/body/eval_jaxpr/dot_general | solution.py:24
  153.3 2.2 fusion.70
  157.5 8.0 %convert_reduce_fusion.5 = (f32[512]{0:T(512)S(1)}, bf16[512,1536]{1,0:T(8,128)(2,1)}, f32[]{:T(128)}) fusion(f32[1536]{0:T(1024)S(1)} %mul.351, f32[512]{0:T(512)S(1)} %bitcast.112, f32[]{:T(128)} %bitcast.97, f32[]{:T(128)} %bitcast.98, f32[]{:T(128)} %bitcast.99, bf16[1536,256]{1,0:T(8,128)(2,1)} %get-tuple-element.400, ...), kind=kOutput, calls=%fused_computation.11.clone.1 | convolution fusion | flops 419167744 | bytes 2641416 | tf_op jit(solution)/shard_map/while/body/eval_jaxpr/dot_general | solution.py:24
  166.0 2.2 fusion.70
  169.3 45.8 %while.27 = (s32[]{:T(128)}, f32[]{:T(128)}, f32[3,512,256]{2,1,0:T(8,128)S(1)}, bf16[3,512,256]{2,1,0:T(8,128)(2,1)}, f32[1536]{0:T(1024)}, /*index=5*/bf16[153...) while((s32[]{:T(128)}, f32[]{:T(128)}, ...), condition=%wide.region_18.19_spmd.clone, body=%wide.region_14.18_spmd.clone.sunk | while | flops 822609920 | bytes 6079325 | solution.py:49
  173.9 7.9 %convert_reduce_fusion.6 = (f32[512]{0:T(512)}, bf16[512,1536]{1,0:T(8,128)(2,1)}, f32[]{:T(128)}) fusion(f32[1536]{0:T(1024)S(1)} %mul.354, f32[512]{0:T(512)S(1)} %bitcast.113, f32[]{:T(128)} %bitcast.108, f32[]{:T(128)} %bitcast.109, f32[]{:T(128)} %bitcast.110, bf16[1536,256]{1,0:T(8,128)(2,1)} %get-tuple-element.370, ...), kind=kOutput, calls=%fused_computation.34.clone.1 | convolution fusion | flops 419167744 | bytes 2643464 | tf_op jit(solution)/shard_map/while/body/eval_jaxpr/dot_general | solution.py:24
  182.3 2.3 fusion.77
  189.1 7.9 %convert_reduce_fusion.6 = (f32[512]{0:T(512)}, bf16[512,1536]{1,0:T(8,128)(2,1)}, f32[]{:T(128)}) fusion(f32[1536]{0:T(1024)S(1)} %mul.354, f32[512]{0:T(512)S(1)} %bitcast.113, f32[]{:T(128)} %bitcast.108, f32[]{:T(128)} %bitcast.109, f32[]{:T(128)} %bitcast.110, bf16[1536,256]{1,0:T(8,128)(2,1)} %get-tuple-element.370, ...), kind=kOutput, calls=%fused_computation.34.clone.1 | convolution fusion | flops 419167744 | bytes 2643464 | tf_op jit(solution)/shard_map/while/body/eval_jaxpr/dot_general | solution.py:24
  197.6 2.3 fusion.77
  204.4 7.9 %convert_reduce_fusion.6 = (f32[512]{0:T(512)}, bf16[512,1536]{1,0:T(8,128)(2,1)}, f32[]{:T(128)}) fusion(f32[1536]{0:T(1024)S(1)} %mul.354, f32[512]{0:T(512)S(1)} %bitcast.113, f32[]{:T(128)} %bitcast.108, f32[]{:T(128)} %bitcast.109, f32[]{:T(128)} %bitcast.110, bf16[1536,256]{1,0:T(8,128)(2,1)} %get-tuple-element.370, ...), kind=kOutput, calls=%fused_computation.34.clone.1 | convolution fusion | flops 419167744 | bytes 2643464 | tf_op jit(solution)/shard_map/while/body/eval_jaxpr/dot_general | solution.py:24
  212.9 2.3 fusion.77
  215.5 19.2 %all_to_all.22 = bf16[32,48,256]{2,1,0:T(8,128)(2,1)S(1)} all-to-all(bf16[32,48,256]{2,1,0:T(8,128)(2,1)S(1)} %bitcast.111), channel_id=1, replica_groups=mesh['dp'=8,'bin'=32] {'bin'}, dimensions={0} | all-to-all | bytes 1572864 | tf_op jit(solution)/shard_map/all_to_all | solution.py:87
  234.7 4.4 %gather_fusion = bf16[768,256]{1,0:T(8,128)(2,1)S(1)} fusion(bf16[32,48,256]{2,1,0:T(8,128)(2,1)S(1)} %all_to_all.22, s32[768]{0:T(1024)S(1)} %get-tuple-element.159), kind=kCustom, calls=%fused_computation | custom fusion | bytes 792576 | tf_op jit(solution)/shard_map/gather | solution.py:90
  240.2 79.6 %psum.23 = f32[]{:T(128)} all-reduce(f32[]{:T(128)S(6)} %add.97), channel_id=1, replica_groups=mesh['dp'=8,'bin'=32] {'dp','bin'}, use_global_device_ids=true, to_apply=%region_21.22 | all-reduce | flops 1 | bytes 8 | tf_op jit(solution)/shard_map/psum | solution.py:99
  321.6 106.0 %all-reduce.5.cloned.1.call-done = f32[256,256]{0,1:T(8,128)} async-done(((f32[256,256]{0,1:T(8,128)}), f32[256,256]{0,1:T(8,128)}) %all-reduce.5.cloned.1.call-update) | async-done | bytes 262160 | tf_op jit(solution)/shard_map/psum | solution.py:102
  (85 shorter events, 35.4 us)
Async XLA Ops:
  7.2 12.8 %copy-start = (bf16[768,256]{1,0:T(8,128)(2,1)S(1)}, bf16[768,256]{1,0:T(8,128)(2,1)}, u32[]{:S(2)}) copy-start(bf16[768,256]{1,0:T(8,128)(2,1)} %param.8) | copy-start | bytes 1179652
  11.6 94.7 %all-to-all-start = ((s32[32,1,1]{2,1,0:T(1,128)}), s32[32,1,1]{2,1,0:T(1,128)S(1)}, u32[]{:S(2)}, u32[]{:S(2)}) async-start(s32[32,1,1]{2,1,0:T(1,128)} %copy.13), calls=%async_computation | async-start | bytes 32768 | tf_op jit(solution)/shard_map/all_to_all | solution.py:69
  106.3 7.5 %copy-start.6 = (f32[3]{0:T(128)S(1)}, f32[3]{0:T(128)}, u32[]{:S(2)}) copy-start(f32[3]{0:T(128)} %param.10) | copy-start | bytes 40
  106.3 20.4 %all-to-all-start.1 = ((bf16[32,48,256]{2,1,0:T(8,128)(2,1)}), bf16[32,48,256]{2,1,0:T(8,128)(2,1)}, u32[]{:S(2)}, u32[]{:S(2)}) async-start(bf16[32,48,256]{2,1,0:T(8,128)(2,1)} %scatter_fusion), calls=%async_computation.1 | async-start | bytes 1572864 | tf_op jit(solution)/shard_map/all_to_all | solution.py:68
  113.7 206.8 %all-reduce.3.cloned.1.call-start = ((), (), s32[]{:S(2)}) async-start(), calls=%async_computation.3 | async-start | bytes 524288 | tf_op jit(solution)/shard_map/psum | solution.py:102
  115.1 10.3 %collective-permute-start = (s32[32,1]{0,1:T(1,128)S(1)}, s32[32,1]{0,1:T(1,128)S(1)}, u32[]{:S(2)}, u32[]{:S(2)}) collective-permute-start(s32[32,1]{0,1:T(1,128)S(1)} %bitcast.115), channel_id=1, source_target_pairs={{0,16},{1,17},{2,18},{3,19},{4,20},{5,21},{6,22},{7,23},{8,24},{9,... | collective-permute-start | bytes 392 | tf_op jit(solution)/shard_map/ppermute | solution.py:10
  126.7 41.6 %collective-permute-start.1 = (bf16[1536,256]{1,0:T(8,128)(2,1)}, bf16[1536,256]{1,0:T(8,128)(2,1)S(1)}, u32[]{:S(2)}, u32[]{:S(2)}) collective-permute-start(bf16[1536,256]{1,0:T(8,128)(2,1)} %bitcast.4), channel_id=1, source_target_pairs={{0,16},{1,17},{2,18},{3,19},{4,20},{5,21},{6,22},{7,23},{8,24},{9,... | collective-permute-start | bytes 2359304 | tf_op jit(solution)/shard_map/ppermute | solution.py:10
  168.3 0.9 copy-start.3
  168.3 0.9 copy-start.1
  169.3 0.6 copy-start.4
  182.3 2.3 copy-start.5
  184.6 0.6 copy-start.4
  197.6 2.3 copy-start.5
  199.9 0.6 copy-start.4
  212.9 2.3 copy-start.5
  239.1 81.5 %copy-start.2 = (bf16[256,256]{1,0:T(8,128)(2,1)S(1)}, bf16[256,256]{1,0:T(8,128)(2,1)}, u32[]{:S(2)}) copy-start(bf16[256,256]{1,0:T(8,128)(2,1)} %param.11) | copy-start | bytes 393220
  240.1 187.5 %all-reduce.5.cloned.1.call-start = ((), (), s32[]{:S(2)}) async-start(), calls=%async_computation.4 | async-start | bytes 524288 | tf_op jit(solution)/shard_map/psum | solution.py:102
Sparse Core Ops, SparseCore 0:
  240.2 73.8 all-reduce.2
  320.7 106.9 all-reduce.4
